TPU v7x, 32 devices: a whole 2x2x4 slice. The times are simulated.
32 devices in a mesh: dp: 8 (over z, y), mp: 4 (over x, core).
Axes of the slice: x: 2, y: 2, z: 4, core: 2. Of those that a mesh axis runs over, the one named last changes fastest.
Arguments:
- tokens: bfloat16 [128, 147, 768], P('dp'), may hold values from -6 to 6
- cotangent: bfloat16 [128, 147, 768], P('dp'), may hold values from -6 to 6
- visible: int32 [128, 147], P('dp'), may hold values from 0 to 587, as said below
- tile_counts: int32 [8], P('dp'), may hold values from 1 to 16, as said below
- attend_weight: float32 [768, 3, 768], P('dp', None, 'mp'), may hold values from -0.3125 to 0.3125
- project_weight: float32 [768, 768], P('mp', 'dp'), may hold values from -0.875 to 0.875
- widen_weight: float32 [768, 3072], P('dp', 'mp'), may hold values from -0.21875 to 0.21875
- narrow_weight: float32 [3072, 768], P('mp', 'dp'), may hold values from -0.109375 to 0.109375
- heads_offset: float32 [2, 12, 64], P(None, 'mp', 'dp'), may hold values from -0.6 to 0.6
- hidden_offset: float32 [48, 64], P('mp', 'dp'), may hold values from -0.6 to 0.6
- layer_vectors: float32 [6, 768], P(None, 'dp'), may hold values from -1 to 2
- attend_first: float32 [768, 3, 768], P('dp', None, 'mp')
- project_first: float32 [768, 768], P('mp', 'dp')
- widen_first: float32 [768, 3072], P('dp', 'mp')
- narrow_first: float32 [3072, 768], P('mp', 'dp')
- heads_first: float32 [2, 12, 64], P(None, 'mp', 'dp')
- hidden_first: float32 [48, 64], P('mp', 'dp')
- vectors_first: float32 [6, 768], P(None, 'dp')
- attend_second: float32 [768, 3, 768], P('dp', None, 'mp')
- project_second: float32 [768, 768], P('mp', 'dp')
- widen_second: float32 [768, 3072], P('dp', 'mp')
- narrow_second: float32 [3072, 768], P('mp', 'dp')
- heads_second: float32 [2, 12, 64], P(None, 'mp', 'dp')
- hidden_second: float32 [48, 64], P('mp', 'dp')
- vectors_second: float32 [6, 768], P(None, 'dp')
Outputs:
- output: bfloat16 [128, 147, 768], P('dp')
- input_grad: float32 [128, 147, 768], P('dp')
- grad_attend: float32 [768, 3, 768], P('dp', None, 'mp')
- grad_project: float32 [768, 768], P('mp', 'dp')
- grad_widen: float32 [768, 3072], P('dp', 'mp')
- grad_narrow: float32 [3072, 768], P('mp', 'dp')
- grad_heads: float32 [2, 12, 64], P(None, 'mp', 'dp')
- grad_hidden: float32 [48, 64], P('mp', 'dp')
- grad_vectors: float32 [6, 768], P(None, 'dp')
- new_attend: float32 [768, 3, 768], P('dp', None, 'mp')
- new_project: float32 [768, 768], P('mp', 'dp')
- new_widen: float32 [768, 3072], P('dp', 'mp')
- new_narrow: float32 [3072, 768], P('mp', 'dp')
- new_heads: float32 [2, 12, 64], P(None, 'mp', 'dp')
- new_hidden: float32 [48, 64], P('mp', 'dp')
- new_vectors: float32 [6, 768], P(None, 'dp')
- first_attend: float32 [768, 3, 768], P('dp', None, 'mp')
- first_project: float32 [768, 768], P('mp', 'dp')
- first_widen: float32 [768, 3072], P('dp', 'mp')
- first_narrow: float32 [3072, 768], P('mp', 'dp')
- first_heads: float32 [2, 12, 64], P(None, 'mp', 'dp')
- first_hidden: float32 [48, 64], P('mp', 'dp')
- first_vectors: float32 [6, 768], P(None, 'dp')
- second_attend: float32 [768, 3, 768], P('dp', None, 'mp')
- second_project: float32 [768, 768], P('mp', 'dp')
- second_widen: float32 [768, 3072], P('dp', 'mp')
- second_narrow: float32 [3072, 768], P('mp', 'dp')
- second_heads: float32 [2, 12, 64], P(None, 'mp', 'dp')
- second_hidden: float32 [48, 64], P('mp', 'dp')
- second_vectors: float32 [6, 768], P(None, 'dp')
- copy_attend: bfloat16 [768, 3, 768], P('dp', None, 'mp')
- copy_project: bfloat16 [768, 768], P('mp', 'dp')
- copy_widen: bfloat16 [768, 3072], P('dp', 'mp')
- copy_narrow: bfloat16 [3072, 768], P('mp', 'dp')
- copy_heads: bfloat16 [2, 12, 64], P(None, 'mp', 'dp')
- copy_hidden: bfloat16 [48, 64], P('mp', 'dp')
- copy_vectors: bfloat16 [6, 768], P(None, 'dp')
Inputs may be any that keep to these rules, and one draw needn't show every extreme that they name: `visible`: the 147 places of one tile are distinct, of 3 frames of 14 x 14 patches. `tile_counts`: slots from this count on hold padding; some device has every slot live and some has one.
All inputs are finite; a program needn't handle non-finite values.
Results may differ from a plain program's by a relative error of at most 0.017.
The roundings to bfloat16 on the way count: a program that leaves them out, or rounds other values in their place, can miss the bound.
Values may be sent and summed in bfloat16 or wider, within the bound.
A program may use at most 192 MiB of HBM per device.

v0:
```python
import math
import jax
import jax.numpy as jnp
from jax import lax
from jax.sharding import PartitionSpec as P

D = 768
FF = 3072
GRID = 14
STEP = 3
LN_EPS = 1e-06
BETA_ONE = 0.5
BETA_TWO = 0.5
ADAM_EPS = 1e-08
DECAY = 0.05


def cut_along(x, dim, size):
    dims = x.shape
    parts = x.reshape(*dims[:dim], size, dims[dim] // size, *dims[dim + 1 :])
    return jnp.moveaxis(parts, dim, 0)


def summed_on_arrival(x, axis, dim):
    size = lax.axis_size(axis)
    parts = lax.all_to_all(cut_along(x, dim, size), axis, 0, 0, tiled=True)
    return jnp.sum(parts.astype(jnp.float32), axis=0)


def sine_table(places, feature_width):
    half_width = feature_width // 2
    spread = jnp.arange(half_width, dtype=jnp.float32) / half_width
    frequency = jnp.exp(-math.log(10000.0) * spread)
    angles = places[..., None] * frequency
    return jnp.concatenate([jnp.sin(angles), jnp.cos(angles)], axis=-1)


def position_table(visible, feature_width):
    plane_size = GRID * GRID
    frame_place = (visible // plane_size).astype(jnp.float32)
    within = visible % plane_size
    row_place = (within // GRID).astype(jnp.float32)
    column_place = (within % GRID).astype(jnp.float32)
    time_width = feature_width // 16 * 4
    space_width = feature_width // 16 * 6
    return jnp.concatenate(
        [
            sine_table(frame_place, time_width),
            sine_table(row_place, space_width),
            sine_table(column_place, space_width),
        ],
        axis=-1,
    )


def normalize(values):
    center = values - jnp.mean(values, axis=-1, keepdims=True)
    inverse = lax.rsqrt(jnp.mean(center * center, axis=-1, keepdims=True) + LN_EPS)
    return (center * inverse, inverse)


def norm_back(grad_normed, normed, inverse):
    return inverse * (
        grad_normed
        - jnp.mean(grad_normed, axis=-1, keepdims=True)
        - normed * jnp.mean(grad_normed * normed, axis=-1, keepdims=True)
    )


def over_rows(former, latter):
    return lax.dot_general(
        former, latter, (((0,), (0,)), ((), ())), preferred_element_type=jnp.float32
    )


def over_cols(former, latter):
    return lax.dot_general(
        former, latter, (((1,), (1,)), ((), ())), preferred_element_type=jnp.float32
    )


def exact_gelu(values):
    return jax.nn.gelu(values, approximate=False)


def adamw_update(
    master, first_moment, second_moment, gradient, step_rate, weight_decay, correction
):
    first_new = BETA_ONE * first_moment + (1.0 - BETA_ONE) * gradient
    second_new = BETA_TWO * second_moment + (1.0 - BETA_TWO) * gradient * gradient
    ratio = first_new / correction / (jnp.sqrt(second_new / correction) + ADAM_EPS)
    master_new = master - step_rate * (ratio + weight_decay * master)
    return (master_new, first_new, second_new)


def shards(
    tokens,
    cotangent,
    visible,
    tile_counts,
    attend_weight,
    project_weight,
    widen_weight,
    narrow_weight,
    heads_offset,
    hidden_offset,
    layer_vectors,
    attend_first,
    project_first,
    widen_first,
    narrow_first,
    heads_first,
    hidden_first,
    vectors_first,
    attend_second,
    project_second,
    widen_second,
    narrow_second,
    heads_second,
    hidden_second,
    vectors_second,
):
    fore_attend, fore_project, fore_widen, fore_narrow, fore_heads, fore_hidden, fore_vectors = (
        lax.all_gather(attend_weight.astype(jnp.bfloat16), "dp", axis=0, tiled=True),
        lax.all_gather(project_weight.astype(jnp.bfloat16), "dp", axis=1, tiled=True),
        lax.all_gather(widen_weight.astype(jnp.bfloat16), "dp", axis=0, tiled=True),
        lax.all_gather(narrow_weight.astype(jnp.bfloat16), "dp", axis=1, tiled=True),
        lax.all_gather(heads_offset.astype(jnp.bfloat16), "dp", axis=2, tiled=True),
        lax.all_gather(hidden_offset.astype(jnp.bfloat16), "dp", axis=1, tiled=True),
        lax.all_gather(layer_vectors.astype(jnp.bfloat16), "dp", axis=1, tiled=True),
    )
    tile_count, seq_length, model_width = tokens.shape
    row_count = tile_count * seq_length
    local_width = fore_attend.shape[2]
    heads_local = fore_heads.shape[1]
    head_size = fore_heads.shape[2]
    score_scale = 1.0 / math.sqrt(head_size)
    live_tiles = (jnp.arange(tile_count, dtype=jnp.int32) < tile_counts[0]).astype(jnp.float32)
    live_rows = jnp.broadcast_to(live_tiles[:, None], (tile_count, seq_length)).reshape(
        row_count, 1
    )
    vectors = fore_vectors.astype(jnp.float32)
    summed = (tokens.astype(jnp.float32) + position_table(visible, model_width)).reshape(
        row_count, model_width
    )
    normed_one, inverse_one = normalize(summed)
    attend_low = (normed_one * vectors[0] + vectors[1]).astype(jnp.bfloat16)
    linear = jnp.dot(
        attend_low,
        fore_attend.reshape(model_width, 3 * local_width),
        preferred_element_type=jnp.float32,
    ).reshape(row_count, 3, local_width)
    offsets = fore_heads.astype(jnp.float32).reshape(2, local_width)
    head_shape = (tile_count, seq_length, heads_local, head_size)
    query_low = (linear[:, 0] + offsets[0]).astype(jnp.bfloat16).reshape(head_shape)
    key_low = linear[:, 1].astype(jnp.bfloat16).reshape(head_shape)
    value_low = (linear[:, 2] + offsets[1]).astype(jnp.bfloat16).reshape(head_shape)
    scores = (
        jnp.einsum("tqhd,tkhd->thqk", query_low, key_low, preferred_element_type=jnp.float32)
        * score_scale
    )
    row_top = jnp.max(scores, axis=-1, keepdims=True)
    log_total = row_top + jnp.log(jnp.sum(jnp.exp(scores - row_top), axis=-1, keepdims=True))
    weights_low = jnp.exp(scores - log_total).astype(jnp.bfloat16)
    context = jnp.einsum(
        "thqk,tkhd->tqhd", weights_low, value_low, preferred_element_type=jnp.float32
    )
    context_low = context.reshape(row_count, local_width).astype(jnp.bfloat16)
    attention_part = jnp.dot(context_low, fore_project, preferred_element_type=jnp.float32)
    attention = lax.psum(attention_part.astype(jnp.bfloat16), "mp").astype(jnp.float32)
    middle = summed + attention + vectors[4]
    normed_two, inverse_two = normalize(middle)
    widen_low = (normed_two * vectors[2] + vectors[3]).astype(jnp.bfloat16)
    hidden = jnp.dot(
        widen_low, fore_widen, preferred_element_type=jnp.float32
    ) + fore_hidden.astype(jnp.float32).reshape(-1)
    active_low = exact_gelu(hidden).astype(jnp.bfloat16)
    feed_part = jnp.dot(active_low, fore_narrow, preferred_element_type=jnp.float32)
    feed_sum = lax.psum(feed_part.astype(jnp.bfloat16), "mp").astype(jnp.float32)
    result = (middle + feed_sum + vectors[5]) * live_rows
    output_low = result.astype(jnp.bfloat16)
    back_attend, back_project, back_widen, back_narrow, back_vectors = (
        fore_attend,
        fore_project,
        fore_widen,
        fore_narrow,
        fore_vectors,
    )
    vectors_back = back_vectors.astype(jnp.float32)
    grad_out = cotangent.astype(jnp.float32).reshape(row_count, model_width) * live_rows
    grad_out_low = grad_out.astype(jnp.bfloat16)
    grad_narrow = over_rows(active_low, grad_out_low)
    grad_active = over_cols(grad_out_low, back_narrow)
    gelu_back = jax.vjp(exact_gelu, hidden)[1]
    grad_hidden_low = gelu_back(grad_active)[0].astype(jnp.bfloat16)
    grad_widen = over_rows(widen_low, grad_hidden_low)
    grad_hidden = jnp.sum(grad_hidden_low.astype(jnp.float32), axis=0).reshape(fore_hidden.shape)
    normed_two_part = over_cols(grad_hidden_low, back_widen)
    grad_normed_two = lax.psum(normed_two_part.astype(jnp.bfloat16), "mp").astype(jnp.float32)
    grad_middle = grad_out + norm_back(grad_normed_two * vectors_back[2], normed_two, inverse_two)
    grad_middle_low = grad_middle.astype(jnp.bfloat16)
    grad_project = over_rows(context_low, grad_middle_low)
    grad_context_low = (
        over_cols(grad_middle_low, back_project).astype(jnp.bfloat16).reshape(head_shape)
    )
    scores_again = (
        jnp.einsum("tqhd,tkhd->thqk", query_low, key_low, preferred_element_type=jnp.float32)
        * score_scale
    )
    weights_full = jnp.exp(scores_again - log_total)
    weights_again_low = weights_full.astype(jnp.bfloat16)
    grad_weights = jnp.einsum(
        "tqhd,tkhd->thqk", grad_context_low, value_low, preferred_element_type=jnp.float32
    )
    grad_value = jnp.einsum(
        "thqk,tqhd->tkhd", weights_again_low, grad_context_low, preferred_element_type=jnp.float32
    )
    row_dot = jnp.sum(grad_weights * weights_full, axis=-1, keepdims=True)
    grad_scores_low = (weights_full * (grad_weights - row_dot)).astype(jnp.bfloat16)
    grad_query = (
        jnp.einsum("thqk,tkhd->tqhd", grad_scores_low, key_low, preferred_element_type=jnp.float32)
        * score_scale
    )
    grad_key = (
        jnp.einsum(
            "thqk,tqhd->tkhd", grad_scores_low, query_low, preferred_element_type=jnp.float32
        )
        * score_scale
    )
    grad_qkv_low = jnp.stack(
        [
            grad_query.reshape(row_count, local_width),
            grad_key.reshape(row_count, local_width),
            grad_value.reshape(row_count, local_width),
        ],
        axis=1,
    ).astype(jnp.bfloat16)
    grad_offsets = jnp.sum(grad_qkv_low.astype(jnp.float32), axis=0)
    grad_heads = jnp.stack([grad_offsets[0], grad_offsets[2]]).reshape(2, heads_local, head_size)
    flat_qkv = grad_qkv_low.reshape(row_count, 3 * local_width)
    grad_attend = over_rows(attend_low, flat_qkv).reshape(model_width, 3, local_width)
    normed_one_part = over_cols(flat_qkv, back_attend.reshape(model_width, 3 * local_width))
    grad_normed_one = lax.psum(normed_one_part.astype(jnp.bfloat16), "mp").astype(jnp.float32)
    grad_inputs = grad_middle + norm_back(
        grad_normed_one * vectors_back[0], normed_one, inverse_one
    )
    grad_vectors = jnp.stack(
        [
            jnp.sum(grad_normed_one * normed_one, axis=0),
            jnp.sum(grad_normed_one, axis=0),
            jnp.sum(grad_normed_two * normed_two, axis=0),
            jnp.sum(grad_normed_two, axis=0),
            jnp.sum(grad_middle, axis=0),
            jnp.sum(grad_out, axis=0),
        ]
    )
    output = output_low.reshape(tile_count, seq_length, model_width)
    input_grad = grad_inputs.reshape(tile_count, seq_length, model_width)
    (
        shard_attend,
        shard_project,
        shard_widen,
        shard_narrow,
        shard_heads,
        shard_hidden,
        shard_vectors,
    ) = (
        summed_on_arrival(grad_attend.astype(jnp.bfloat16), "dp", 0),
        summed_on_arrival(grad_project.astype(jnp.bfloat16), "dp", 1),
        summed_on_arrival(grad_widen.astype(jnp.bfloat16), "dp", 0),
        summed_on_arrival(grad_narrow.astype(jnp.bfloat16), "dp", 1),
        summed_on_arrival(grad_heads.astype(jnp.bfloat16), "dp", 2),
        summed_on_arrival(grad_hidden.astype(jnp.bfloat16), "dp", 1),
        summed_on_arrival(grad_vectors.astype(jnp.bfloat16), "dp", 1),
    )
    correction = 1.0 - 0.5**STEP
    new_attend, first_attend, second_attend = adamw_update(
        attend_weight,
        attend_first,
        attend_second,
        shard_attend,
        (D // 2) ** (-0.5),
        DECAY,
        correction,
    )
    new_project, first_project, second_project = adamw_update(
        project_weight,
        project_first,
        project_second,
        shard_project,
        (D // 16) ** (-0.5),
        DECAY,
        correction,
    )
    new_widen, first_widen, second_widen = adamw_update(
        widen_weight, widen_first, widen_second, shard_widen, D ** (-0.5), DECAY, correction
    )
    new_narrow, first_narrow, second_narrow = adamw_update(
        narrow_weight, narrow_first, narrow_second, shard_narrow, FF ** (-0.5), DECAY, correction
    )
    new_heads, first_heads, second_heads = adamw_update(
        heads_offset, heads_first, heads_second, shard_heads, 0.1, 0.0, correction
    )
    new_hidden, first_hidden, second_hidden = adamw_update(
        hidden_offset, hidden_first, hidden_second, shard_hidden, 0.1, 0.0, correction
    )
    new_vectors, first_vectors, second_vectors = adamw_update(
        layer_vectors, vectors_first, vectors_second, shard_vectors, 0.15, 0.0, correction
    )
    return (
        output,
        input_grad,
        shard_attend,
        shard_project,
        shard_widen,
        shard_narrow,
        shard_heads,
        shard_hidden,
        shard_vectors,
        new_attend,
        new_project,
        new_widen,
        new_narrow,
        new_heads,
        new_hidden,
        new_vectors,
        first_attend,
        first_project,
        first_widen,
        first_narrow,
        first_heads,
        first_hidden,
        first_vectors,
        second_attend,
        second_project,
        second_widen,
        second_narrow,
        second_heads,
        second_hidden,
        second_vectors,
        new_attend.astype(jnp.bfloat16),
        new_project.astype(jnp.bfloat16),
        new_widen.astype(jnp.bfloat16),
        new_narrow.astype(jnp.bfloat16),
        new_heads.astype(jnp.bfloat16),
        new_hidden.astype(jnp.bfloat16),
        new_vectors.astype(jnp.bfloat16),
    )


def solution(mesh):
    in_specs = (
        P("dp", None, None),
        P("dp", None, None),
        P("dp", None),
        P("dp"),
        P("dp", None, "mp"),
        P("mp", "dp"),
        P("dp", "mp"),
        P("mp", "dp"),
        P(None, "mp", "dp"),
        P("mp", "dp"),
        P(None, "dp"),
        P("dp", None, "mp"),
        P("mp", "dp"),
        P("dp", "mp"),
        P("mp", "dp"),
        P(None, "mp", "dp"),
        P("mp", "dp"),
        P(None, "dp"),
        P("dp", None, "mp"),
        P("mp", "dp"),
        P("dp", "mp"),
        P("mp", "dp"),
        P(None, "mp", "dp"),
        P("mp", "dp"),
        P(None, "dp"),
    )
    out_specs = (
        P("dp", None, None),
        P("dp", None, None),
        P("dp", None, "mp"),
        P("mp", "dp"),
        P("dp", "mp"),
        P("mp", "dp"),
        P(None, "mp", "dp"),
        P("mp", "dp"),
        P(None, "dp"),
        P("dp", None, "mp"),
        P("mp", "dp"),
        P("dp", "mp"),
        P("mp", "dp"),
        P(None, "mp", "dp"),
        P("mp", "dp"),
        P(None, "dp"),
        P("dp", None, "mp"),
        P("mp", "dp"),
        P("dp", "mp"),
        P("mp", "dp"),
        P(None, "mp", "dp"),
        P("mp", "dp"),
        P(None, "dp"),
        P("dp", None, "mp"),
        P("mp", "dp"),
        P("dp", "mp"),
        P("mp", "dp"),
        P(None, "mp", "dp"),
        P("mp", "dp"),
        P(None, "dp"),
        P("dp", None, "mp"),
        P("mp", "dp"),
        P("dp", "mp"),
        P("mp", "dp"),
        P(None, "mp", "dp"),
        P("mp", "dp"),
        P(None, "dp"),
    )
    return jax.shard_map(shards, mesh=mesh, in_specs=in_specs, out_specs=out_specs, check_vma=False)
```

profile of v0, /device:TPU:0, one launch (start us, length us, event | category | flops | bytes accessed | tf_op | source)
XLA Modules:
  0.0 817.2 jit_solution(17125010776778953683)
XLA Ops:
  8.8 27.9 %all-gather = bf16[8,96,6]{1,2,0:T(8,128)(2,1)S(1)} all-gather(bf16[1,96,6]{1,2,0:T(8,128)(2,1)S(1)} %convert_bitcast_fusion), channel_id=1, replica_groups=mesh['dp'=8,'mp'=4] {'dp'}, dimensions={0}, use_global_device_ids=true | all-gather | bytes 10368 | tf_op jit(solution)/shard_map/all_gather | solution.py:130
  39.5 33.2 %all_gather.22 = bf16[768,3,192]{2,0,1:T(8,128)(2,1)S(1)} all-gather(bf16[96,3,192]{2,0,1:T(8,128)(2,1)S(1)} %convert_element_type.217), channel_id=1, replica_groups=mesh['dp'=8,'mp'=4] {'dp'}, dimensions={0}, use_global_device_ids=true | all-gather | bytes 995328 | tf_op jit(solution)/shard_map/all_gather | solution.py:124
  79.4 19.3 %multiply_cosine_fusion = (f32[16,147,144]{2,0,1:T(8,128)S(1)}, f32[16,147,144]{2,0,1:T(8,128)}, f32[16,147,144]{2,0,1:T(8,128)}, f32[16,147,144]{2,0,1:T(8,128)}) fusion(f32[16,147]{0,1:T(8,128)S(1)} %copy.347, f32[144]{0:T(256)S(1)} %multiply_exponential_fusion, f32[16,147]{0,1:T(8,128)S(1)} %copy.346), kind=kLoop, calls=%fused_computation.60 | loop fusion | flops 677376 | bytes 5438400 | tf_op jit(solution)/shard_map/cos | solution.py:35
  98.7 11.6 %concatenate.5 = f32[16,147,768]{2,0,1:T(8,128)} concatenate(f32[16,147,96]{2,0,1:T(8,128)} %get-tuple-element.356, f32[16,147,96]{2,0,1:T(8,128)} %get-tuple-element.355, f32[16,147,144]{2,0,1:T(8,128)} %get-tuple-element.364, f32[16,147,144]{2,0,1:T(8,128)} %get-tuple-element.365, f32[16,147,144]{2,0,1:T(8,128)} %get-tuple-element.352, f32[16,147,144]{2,0,1:T(8,128)S(1)} %get-tuple-element.351), dimensions={2} | concatenate | bytes 14450688 | tf_op jit(solution)/shard_map/concatenate | solution.py:46
  110.3 7.8 fusion.87
  140.7 30.6 %all_gather.23 = bf16[2,3,64]{1,0,2:T(2,128)(2,1)S(1)} all-gather(bf16[2,3,8]{1,0,2:T(2,128)(2,1)S(1)} %copy.356), channel_id=1, replica_groups=mesh['dp'=8,'mp'=4] {'dp'}, dimensions={2}, use_global_device_ids=true | all-gather | bytes 864 | tf_op jit(solution)/shard_map/all_gather | solution.py:128
  171.6 31.4 %all_gather.24 = bf16[192,768]{0,1:T(8,128)(2,1)S(1)} all-gather(bf16[192,96]{0,1:T(8,128)(2,1)S(1)} %copy.364), channel_id=1, replica_groups=mesh['dp'=8,'mp'=4] {'dp'}, dimensions={1}, use_global_device_ids=true | all-gather | bytes 331776 | tf_op jit(solution)/shard_map/all_gather | solution.py:125
  243.8 12.3 %all-gather.6.cloned.1.call-start = ((), (), s32[]{:S(2)}) async-start(), calls=%async_computation.9 | async-start | bytes 1327104 | tf_op jit(solution)/shard_map/all_gather | solution.py:127
  256.1 10.4 %copy.348 = f32[16,147,768]{2,1,0:T(8,128)} copy(f32[16,147,768]{2,0,1:T(8,128)} %get-tuple-element.347) | data formatting | bytes 14450688 | tf_op jit(solution)/shard_map/add | solution.py:143
  267.7 26.3 %all_gather.26 = bf16[12,64]{0,1:T(8,128)(2,1)S(1)} all-gather(bf16[12,8]{0,1:T(8,128)(2,1)S(1)} %convert_element_type.232), channel_id=1, replica_groups=mesh['dp'=8,'mp'=4] {'dp'}, dimensions={1}, use_global_device_ids=true | all-gather | bytes 1728 | tf_op jit(solution)/shard_map/all_gather | solution.py:129
  329.4 21.0 %multiply_convert_fusion.2 = (bf16[2352,768]{1,0:T(8,128)(2,1)S(1)}, f32[2352,768]{1,0:T(8,128)}, f32[2352,768]{1,0:T(8,128)}) fusion(f32[768]{0:T(1024)} %reshape.311, bf16[2352,768]{1,0:T(8,128)(2,1)} %add_convert_fusion.1, bf16[768,768]{1,0:T(8,128)(2,1)} %all-gather.4.cloned.1.call-done), kind=kOutput, calls=%fused_computation.31 | convolution fusion | flops 2893750272 | bytes 22858752 | tf_op jit(solution)/shard_map/dot_general | solution.py:174
  350.4 7.9 convolution_convert_fusion.5
  358.3 34.1 %all_to_all.35 = bf16[8,768,96]{1,2,0:T(8,128)(2,1)S(1)} all-to-all(bf16[8,768,96]{1,2,0:T(8,128)(2,1)S(1)} %bitcast.97), channel_id=1, replica_groups=mesh['dp'=8,'mp'=4] {'dp'}, dimensions={0} | all-to-all | bytes 2359296 | tf_op jit(solution)/shard_map/all_to_all | solution.py:26
  394.6 39.3 %all-gather.6.cloned.1.call-done = bf16[768,768]{0,1:T(8,128)(2,1)} async-done(((bf16[768,96]{0,1:T(8,128)(2,1)}), bf16[768,768]{0,1:T(8,128)(2,1)}) %all-gather.6.cloned.1.call-update) | async-done | bytes 1179664 | tf_op jit(solution)/shard_map/all_gather | solution.py:127
  433.9 11.3 %fusion.91 = (bf16[768]{0:T(1024)(128)(2,1)}, bf16[2352,768]{1,0:T(8,128)(2,1)S(1)}) fusion(f32[2352,768]{1,0:T(8,128)} %get-tuple-element.343, bf16[768,768]{0,1:T(8,128)(2,1)} %all-gather.6.cloned.1.call-done, f32[2352,768]{1,0:T(8,128)} %reshape.304, f32[2352]{0:T(1024)} %mul.444, f32[2352,768]{1,0:T(8,128)} %get-tuple-element.368, f32[768]{0:T(1024)} %reshape.311), kind=kOutput, calls=%fused_computation.191 | convolution fusion | flops 2807045376 | bytes 26482368 | tf_op jit(solution)/shard_map/dot_general | solution.py:77
  458.3 68.1 %all-reduce.7.cloned.1.call-done = bf16[2352,768]{1,0:T(8,128)(2,1)} async-done(((bf16[2352,768]{1,0:T(8,128)(2,1)}), bf16[2352,768]{1,0:T(8,128)(2,1)}) %all-reduce.7.cloned.1.call-update) | async-done | bytes 3612688 | tf_op jit(solution)/shard_map/psum | solution.py:199
  526.4 7.8 fusion.10
  534.2 7.6 fusion.82
  594.6 7.5 convolution_convert_fusion.6
  626.9 9.3 %all-to-all-done.2 = bf16[8,96,768]{2,1,0:T(8,128)(2,1)S(1)} async-done(((bf16[8,96,768]{2,1,0:T(8,128)(2,1)}), bf16[8,96,768]{2,1,0:T(8,128)(2,1)S(1)}, u32[]{:S(2)}, u32[]{:S(2)}) %all-to-all-start.2) | async-done | bytes 1179680 | tf_op jit(solution)/shard_map/all_to_all | solution.py:26
  675.7 8.8 %all-to-all-done = bf16[8,96,3,192]{1,3,2,0:T(8,128)(2,1)S(1)} async-done(((bf16[8,96,3,192]{1,3,2,0:T(8,128)(2,1)}), bf16[8,96,3,192]{1,3,2,0:T(8,128)(2,1)S(1)}, u32[]{:S(2)}, u32[]{:S(2)}) %all-to-all-start) | async-done | bytes 884768 | tf_op jit(solution)/shard_map/all_to_all | solution.py:26
  690.4 65.6 %all-reduce.9.cloned.1.call-done = (bf16[2352,768]{1,0:T(8,128)(2,1)}, bf16[2352,768]{1,0:T(8,128)(2,1)}) async-done(((bf16[2352,768]{1,0:T(8,128)(2,1)}, bf16[2352,768]{1,0:T(8,128)(2,1)}), (bf16[2352,768]{1,0:T(8,128)(2,1)}, bf16[2352,768]{1,0:T(8,128)(2,1)})) %all-reduce.9.cloned.1.call-update) | async-done | bytes 7225360 | tf_op jit(solution)/shard_map/psum | solution.py:179
  772.5 11.5 %fusion.13 = f32[2352,768]{1,0:T(8,128)} fusion(f32[2352,768]{1,0:T(8,128)} %copy-done.2, bf16[2352,768]{1,0:T(8,128)(2,1)} %get-tuple-element.309, f32[2352,768]{1,0:T(8,128)} %reshape.301, f32[2352]{0:T(1024)S(1)} %broadcast_multiply_fusion.1, f32[2352]{0:T(1024)S(1)} %div.112, f32[2352]{0:T(1024)S(1)} %broadcast_multiply_fusion.2, f32[768]{0:T(1024)S(1)} %copy-done.35, ...), kind=kLoop, calls=%fused_computation.22 | loop fusion | flops 16257024 | bytes 25329408 | tf_op jit(solution)/shard_map/add | solution.py:244
  800.7 8.5 %copy.396 = f32[16,147,768]{2,0,1:T(8,128)} copy(f32[16,147,768]{2,1,0:T(8,128)} %reshape.306) | data formatting | bytes 14450688
  (296 shorter events, 281.1 us)
Async XLA Ops:
  8.0 310.5 %all-reduce.5.cloned.1.call-start = ((), (), s32[]{:S(2)}) async-start(), calls=%async_computation.7 | async-start | bytes 7225344 | tf_op jit(solution)/shard_map/psum | solution.py:170
  37.5 85.6 %copy-start.34 = (f32[768]{0:T(1024)}, f32[768]{0:T(1024)S(1)}, u32[]{:S(2)}) copy-start(f32[768]{0:T(1024)S(1)} %get-tuple-element.307) | copy-start | bytes 9220
  138.3 33.1 %copy-start.17 = (f32[192,96]{1,0:T(8,128)S(1)}, f32[192,96]{1,0:T(8,128)}, u32[]{:S(2)}) copy-start(f32[192,96]{1,0:T(8,128)} %param.30) | copy-start | bytes 221188
  171.4 56.1 %copy-start.39 = (f32[1,3,64]{2,1,0:T(4,128)}, f32[1,3,64]{2,1,0:T(4,128)S(1)}, u32[]{:S(2)}) copy-start(f32[1,3,64]{2,1,0:T(4,128)S(1)} %copy.357) | copy-start | bytes 2308
  171.5 54.3 %copy-start.37 = (f32[1,3,64]{2,1,0:T(4,128)}, f32[1,3,64]{2,1,0:T(4,128)S(1)}, u32[]{:S(2)}) copy-start(f32[1,3,64]{2,1,0:T(4,128)S(1)} %copy.359) | copy-start | bytes 2308
  242.1 87.3 %all-gather.4.cloned.1.call-start = ((), (), s32[]{:S(2)}) async-start(), calls=%async_computation.8 | async-start | bytes 1327104 | tf_op jit(solution)/shard_map/all_gather | solution.py:126
  243.8 23.9 %copy-start.46 = (f32[12,8]{0,1:T(8,128)S(1)}, f32[12,8]{0,1:T(8,128)}, u32[]{:S(2)}) copy-start(f32[12,8]{0,1:T(8,128)} %param.34) | copy-start | bytes 1156
  243.8 190.0 %all-gather.6.cloned.1.call-start = ((), (), s32[]{:S(2)}) async-start(), calls=%async_computation.9 | async-start | bytes 1327104 | tf_op jit(solution)/shard_map/all_gather | solution.py:127
  350.4 42.9 %copy-start.20 = (f32[768,96]{0,1:T(8,128)S(1)}, f32[768,96]{0,1:T(8,128)}, u32[]{:S(2)}) copy-start(f32[768,96]{0,1:T(8,128)} %param.32) | copy-start | bytes 884740
  350.4 42.9 %copy-start.21 = (f32[768,96]{0,1:T(8,128)S(1)}, f32[768,96]{0,1:T(8,128)}, u32[]{:S(2)}) copy-start(f32[768,96]{0,1:T(8,128)} %param.39) | copy-start | bytes 884740
  350.4 42.9 %copy-start.22 = (f32[768,96]{0,1:T(8,128)S(1)}, f32[768,96]{0,1:T(8,128)}, u32[]{:S(2)}) copy-start(f32[768,96]{0,1:T(8,128)} %param.46) | copy-start | bytes 884740
  394.5 131.9 %all-reduce.7.cloned.1.call-start = ((), (), s32[]{:S(2)}) async-start(), calls=%async_computation.10 | async-start | bytes 7225344 | tf_op jit(solution)/shard_map/psum | solution.py:199
  454.4 134.5 %all-to-all-start.5 = ((bf16[8,12,8]{1,2,0:T(8,128)(2,1)}), bf16[8,12,8]{1,2,0:T(8,128)(2,1)}, u32[]{:S(2)}, u32[]{:S(2)}) async-start(bf16[8,12,8]{1,2,0:T(8,128)(2,1)} %copy.382), calls=%async_computation.5 | async-start | bytes 32768 | tf_op jit(solution)/shard_map/all_to_all | solution.py:26
  588.9 13.3 %all-to-all-start.4 = ((bf16[8,2,3,8]{3,1,2,0:T(2,128)(2,1)}), bf16[8,2,3,8]{3,1,2,0:T(2,128)(2,1)S(1)}, u32[]{:S(2)}, u32[]{:S(2)}) async-start(bf16[8,2,3,8]{3,1,2,0:T(2,128)(2,1)} %copy.379), calls=%async_computation.4 | async-start | bytes 24576 | tf_op jit(solution)/shard_map/all_to_all | solution.py:26
  602.1 34.1 %all-to-all-start.2 = ((bf16[8,96,768]{2,1,0:T(8,128)(2,1)}), bf16[8,96,768]{2,1,0:T(8,128)(2,1)S(1)}, u32[]{:S(2)}, u32[]{:S(2)}) async-start(bf16[8,96,768]{2,1,0:T(8,128)(2,1)} %bitcast.18), calls=%async_computation.2 | async-start | bytes 2359296 | tf_op jit(solution)/shard_map/all_to_all | solution.py:26
  608.2 147.9 %all-reduce.9.cloned.1.call-start = ((), (), s32[]{:S(2)}) async-start(), calls=%async_computation.11 | async-start | bytes 14450688 | tf_op jit(solution)/shard_map/psum | solution.py:179
  636.2 15.6 %all-to-all-start.1 = ((bf16[8,192,96]{2,1,0:T(8,128)(2,1)}), bf16[8,192,96]{2,1,0:T(8,128)(2,1)S(1)}, u32[]{:S(2)}, u32[]{:S(2)}) async-start(bf16[8,192,96]{2,1,0:T(8,128)(2,1)} %bitcast.91), calls=%async_computation.1 | async-start | bytes 786432 | tf_op jit(solution)/shard_map/all_to_all | solution.py:26
  649.0 23.5 %copy-start.14 = (f32[96,768]{1,0:T(8,128)S(1)}, f32[96,768]{1,0:T(8,128)}, u32[]{:S(2)}) copy-start(f32[96,768]{1,0:T(8,128)} %param.31) | copy-start | bytes 884740
  651.8 32.7 %all-to-all-start = ((bf16[8,96,3,192]{1,3,2,0:T(8,128)(2,1)}), bf16[8,96,3,192]{1,3,2,0:T(8,128)(2,1)S(1)}, u32[]{:S(2)}, u32[]{:S(2)}) async-start(bf16[8,96,3,192]{1,3,2,0:T(8,128)(2,1)} %copy.376), calls=%async_computation | async-start | bytes 2359296 | tf_op jit(solution)/shard_map/all_to_all | solution.py:26
  665.9 24.6 %copy-start.44 = (f32[12,8]{0,1:T(8,128)}, f32[12,8]{0,1:T(8,128)S(1)}, u32[]{:S(2)}) copy-start(f32[12,8]{0,1:T(8,128)S(1)} %convert_reduce_fusion.5) | copy-start | bytes 1156
  672.3 86.4 %copy-start.35 = (f32[768]{0:T(1024)S(1)}, f32[768]{0:T(1024)}, u32[]{:S(2)}) copy-start(f32[768]{0:T(1024)} %copy-done.34) | copy-start | bytes 9220
  674.9 91.1 %copy-start.19 = (f32[192,96]{1,0:T(8,128)}, f32[192,96]{1,0:T(8,128)S(1)}, u32[]{:S(2)}) copy-start(f32[192,96]{1,0:T(8,128)S(1)} %convert_reduce_fusion.3) | copy-start | bytes 221188
  758.7 25.3 %slice-start.2 = ((s8[7225344]{0:T(1024)(128)(4,1)}), s8[3031040]{0:T(1024)(128)(4,1)S(1)}, s32[]{:S(2)}) async-start(s8[7225344]{0:T(1024)(128)(4,1)} %bitcast.95), calls=%async_computation.14 | async-start | bytes 6062080
  766.7 42.5 %all-to-all-start.6 = ((bf16[8,6,96]{2,1,0:T(8,128)(2,1)}), bf16[8,6,96]{2,1,0:T(8,128)(2,1)S(1)}, u32[]{:S(2)}, u32[]{:S(2)}) async-start(bf16[8,6,96]{2,1,0:T(8,128)(2,1)} %copy.384), calls=%async_computation.6 | async-start | bytes 32768 | tf_op jit(solution)/shard_map/all_to_all | solution.py:26
  (54 other events, 518.5 us)
Sparse Core Ops, SparseCore 0:
  242.2 76.3 all-reduce.4
  451.7 74.6 all-reduce.6
  620.6 135.3 all-reduce.8
Sparse Core Ops, SparseCore 1:
  245.3 41.3 all-gather.3
  394.6 39.2 all-gather.5
where the time goes:
time: 827 us; the launch traced here: 817 us
  waiting for transfers between devices  197 us (24%)
  blocking collectives  183 us (22%)
  local copies, waits for them, and re-layouts  151 us (18%)
  other arithmetic  114 us (14%)
  matrix products  112 us (14%)
  starting transfers between devices  42.1 us (5%)
  between operations  17 us (2%)
    psum x1, waiting for transfers between devices, shards(): lax.psum(normed_two_part.astype(jnp.bfloat16), 'mp').astype(jnp.float32)  68.1 us
    psum x1, waiting for transfers between devices, shards(): lax.psum(feed_part.astype(jnp.bfloat16), 'mp').astype(jnp.float32)  65.6 us
    all_gather x1, waiting for transfers between devices, shards(): lax.all_gather(narrow_weight.astype(jnp.bfloat16), 'dp', axis=1, tiled=True)  39.3 us
    unnamed x155, local copies, waits for them, and re-layouts  36.8 us
    all_to_all x1, blocking collectives, summed_on_arrival(): parts = lax.all_to_all(cut_along(x, dim, size), axis, 0, 0, tiled=True)  34.1 us
    all_gather x1, blocking collectives, shards(): lax.all_gather(attend_weight.astype(jnp.bfloat16), 'dp', axis=0, tiled=True)  33.2 us
    all_gather x1, blocking collectives, shards(): lax.all_gather(project_weight.astype(jnp.bfloat16), 'dp', axis=1, tiled=T...  31.4 us
    all_gather x1, blocking collectives, shards(): lax.all_gather(heads_offset.astype(jnp.bfloat16), 'dp', axis=2, tiled=True)  30.6 us
  transfers between devices with their start and end apart: 11, of which 7 were waited for; matrix products, arithmetic and copies ran while one was open for 25% of the time, Pallas kernels for 0%

commit v1 on v0

--- a/solution.py
+++ b/solution.py
@@ -13,6 +13,24 @@
 BETA_TWO = 0.5
 ADAM_EPS = 1e-08
 DECAY = 0.05
+
+
+def gather_around(array, axis, dim):
+    ways, here, turn = (lax.axis_size(axis), lax.axis_index(axis), array.shape[dim])
+    dims = [n * ways if d == dim else n for d, n in enumerate(array.shape)]
+    full = lax.dynamic_update_slice_in_dim(
+        jnp.zeros(dims, array.dtype), array, here * turn, axis=dim
+    )
+    going_up = going_down = array
+    for far in range(1, ways // 2 + 1):
+        going_up = lax.ppermute(going_up, axis, [(d, (d + 1) % ways) for d in range(ways)])
+        full = lax.dynamic_update_slice_in_dim(full, going_up, (here - far) % ways * turn, axis=dim)
+        if 2 * far < ways:
+            going_down = lax.ppermute(going_down, axis, [(d, (d - 1) % ways) for d in range(ways)])
+            full = lax.dynamic_update_slice_in_dim(
+                full, going_down, (here + far) % ways * turn, axis=dim
+            )
+    return full
 
 
 def cut_along(x, dim, size):
@@ -124,7 +142,7 @@
         lax.all_gather(attend_weight.astype(jnp.bfloat16), "dp", axis=0, tiled=True),
         lax.all_gather(project_weight.astype(jnp.bfloat16), "dp", axis=1, tiled=True),
         lax.all_gather(widen_weight.astype(jnp.bfloat16), "dp", axis=0, tiled=True),
-        lax.all_gather(narrow_weight.astype(jnp.bfloat16), "dp", axis=1, tiled=True),
+        gather_around(narrow_weight.astype(jnp.bfloat16), "dp", 1),
         lax.all_gather(heads_offset.astype(jnp.bfloat16), "dp", axis=2, tiled=True),
         lax.all_gather(hidden_offset.astype(jnp.bfloat16), "dp", axis=1, tiled=True),
         lax.all_gather(layer_vectors.astype(jnp.bfloat16), "dp", axis=1, tiled=True),

time: 827 us -> 787 us (0.952)
  blocking collectives: 183 us -> 149 us
  waiting for transfers between devices: 197 us -> 167 us
  starting transfers between devices: 42.1 us -> 52.5 us
  local copies, waits for them, and re-layouts: 151 us -> 161 us
    all_gather x1 -> x0, waiting for transfers between devices: 39.3 us -> none  [shards(): lax.all_gather(narrow_weight.astype(jnp.bfloat16), 'dp', axis=1, tiled=True)]
    all_to_all x1 -> x0, blocking collectives: 34.1 us -> none  [summed_on_arrival(): parts = lax.all_to_all(cut_along(x, dim, size), axis, 0, 0, tiled=True)]
    all_to_all x6 -> x7, waiting for transfers between devices: 19.7 us -> 37.6 us  [summed_on_arrival(): parts = lax.all_to_all(cut_along(x, dim, size), axis, 0, 0, tiled=True)]
    ppermute x0 -> x7, starting transfers between devices: none -> 14.4 us  [the longest x3 13.6 us: gather_around(): lax.ppermute(going_down, axis, [(d, (d - 1) % ways) for d in range(ways)])]
    all_gather x1 -> x0, starting transfers between devices: 12.3 us -> none  [shards(): lax.all_gather(narrow_weight.astype(jnp.bfloat16), 'dp', axis=1, tiled=True)]
    psum x1, waiting for transfers between devices: 65.6 us -> 54.7 us  [shards(): lax.psum(feed_part.astype(jnp.bfloat16), 'mp').astype(jnp.float32)]
    ppermute x0 -> x7, waiting for transfers between devices: none -> 8.35 us  [the longest x4 8.34 us: gather_around(): lax.ppermute(going_up, axis, [(d, (d + 1) % ways) for d in range(ways)])]
    all_to_all x6 -> x7, starting transfers between devices: 29.6 us -> 37.3 us  [summed_on_arrival(): parts = lax.all_to_all(cut_along(x, dim, size), axis, 0, 0, tiled=True)]
  transfers between devices with their start and end apart: 11 -> 18, of which waited for: 7 -> 7; matrix products, arithmetic and copies ran while one was open for 25% -> 29% of each run, Pallas kernels for 0% -> 0%
where the time goes in v1:
time: 787 us; the launch traced here: 778 us
  waiting for transfers between devices  167 us (21%)
  local copies, waits for them, and re-layouts  161 us (20%)
  blocking collectives  149 us (19%)
  other arithmetic  119 us (15%)
  matrix products  110 us (14%)
  starting transfers between devices  52.5 us (7%)
  between operations  17.4 us (2%)
    psum x1, waiting for transfers between devices, shards(): lax.psum(normed_two_part.astype(jnp.bfloat16), 'mp').astype(jnp.float32)  66.6 us
    psum x1, waiting for transfers between devices, shards(): lax.psum(feed_part.astype(jnp.bfloat16), 'mp').astype(jnp.float32)  54.7 us
    all_to_all x7, waiting for transfers between devices, summed_on_arrival(): parts = lax.all_to_all(cut_along(x, dim, size), axis, 0, 0, tiled=True)  37.6 us
    all_to_all x7, starting transfers between devices, summed_on_arrival(): parts = lax.all_to_all(cut_along(x, dim, size), axis, 0, 0, tiled=True)  37.3 us
    unnamed x151, local copies, waits for them, and re-layouts  36 us
    all_gather x1, blocking collectives, shards(): lax.all_gather(attend_weight.astype(jnp.bfloat16), 'dp', axis=0, tiled=True)  33.2 us
    all_gather x1, blocking collectives, shards(): lax.all_gather(project_weight.astype(jnp.bfloat16), 'dp', axis=1, tiled=T...  31.2 us
    all_gather x1, blocking collectives, shards(): lax.all_gather(heads_offset.astype(jnp.bfloat16), 'dp', axis=2, tiled=True)  30.6 us
  transfers between devices with their start and end apart: 18, of which 7 were waited for; matrix products, arithmetic and copies ran while one was open for 29% of the time, Pallas kernels for 0%

profile of v1, /device:TPU:0, one launch (start us, length us, event | category | flops | bytes accessed | tf_op | source)
XLA Modules:
  0.0 777.6 jit_solution(9186950316923443705)
XLA Ops:
  8.8 27.9 %all-gather = bf16[8,96,6]{1,2,0:T(8,128)(2,1)S(1)} all-gather(bf16[1,96,6]{1,2,0:T(8,128)(2,1)S(1)} %convert_bitcast_fusion), channel_id=1, replica_groups=mesh['dp'=8,'mp'=4] {'dp'}, dimensions={0}, use_global_device_ids=true | all-gather | bytes 10368 | tf_op jit(solution)/shard_map/all_gather | solution.py:148
  39.5 33.2 %all_gather.19 = bf16[768,3,192]{2,0,1:T(8,128)(2,1)S(1)} all-gather(bf16[96,3,192]{2,0,1:T(8,128)(2,1)S(1)} %convert_element_type.217), channel_id=1, replica_groups=mesh['dp'=8,'mp'=4] {'dp'}, dimensions={0}, use_global_device_ids=true | all-gather | bytes 995328 | tf_op jit(solution)/shard_map/all_gather | solution.py:142
  79.4 19.3 %multiply_cosine_fusion = (f32[16,147,144]{2,0,1:T(8,128)S(1)}, f32[16,147,144]{2,0,1:T(8,128)}, f32[16,147,144]{2,0,1:T(8,128)}, f32[16,147,144]{2,0,1:T(8,128)}) fusion(f32[16,147]{0,1:T(8,128)S(1)} %copy.347, f32[144]{0:T(256)S(1)} %multiply_exponential_fusion, f32[16,147]{0,1:T(8,128)S(1)} %copy.346), kind=kLoop, calls=%fused_computation.60 | loop fusion | flops 677376 | bytes 5438400 | tf_op jit(solution)/shard_map/cos | solution.py:53
  98.7 11.6 %concatenate.5 = f32[16,147,768]{2,0,1:T(8,128)} concatenate(f32[16,147,96]{2,0,1:T(8,128)} %get-tuple-element.357, f32[16,147,96]{2,0,1:T(8,128)} %get-tuple-element.356, f32[16,147,144]{2,0,1:T(8,128)} %get-tuple-element.365, f32[16,147,144]{2,0,1:T(8,128)} %get-tuple-element.366, f32[16,147,144]{2,0,1:T(8,128)} %get-tuple-element.353, f32[16,147,144]{2,0,1:T(8,128)S(1)} %get-tuple-element.352), dimensions={2} | concatenate | bytes 14450688 | tf_op jit(solution)/shard_map/concatenate | solution.py:64
  110.3 7.8 %fusion.87 = (f32[16,147]{0,1:T(8,128)S(1)}, f32[16,147,768]{2,0,1:T(8,128)}) fusion(f32[16,147,768]{2,0,1:T(8,128)} %concatenate.5, bf16[16,147,768]{2,0,1:T(8,128)(2,1)} %param.25), kind=kLoop, calls=%fused_computation.195 | loop fusion | flops 5416656 | bytes 18072768 | tf_op jit(solution)/shard_map/reduce_sum | solution.py:75
  140.6 30.6 %all_gather.20 = bf16[2,3,64]{1,0,2:T(2,128)(2,1)S(1)} all-gather(bf16[2,3,8]{1,0,2:T(2,128)(2,1)S(1)} %copy.356), channel_id=1, replica_groups=mesh['dp'=8,'mp'=4] {'dp'}, dimensions={2}, use_global_device_ids=true | all-gather | bytes 864 | tf_op jit(solution)/shard_map/all_gather | solution.py:146
  171.5 31.2 %all_gather.21 = bf16[192,768]{0,1:T(8,128)(2,1)S(1)} all-gather(bf16[192,96]{0,1:T(8,128)(2,1)S(1)} %copy.364), channel_id=1, replica_groups=mesh['dp'=8,'mp'=4] {'dp'}, dimensions={1}, use_global_device_ids=true | all-gather | bytes 331776 | tf_op jit(solution)/shard_map/all_gather | solution.py:143
  251.5 10.3 %copy.348 = f32[16,147,768]{2,1,0:T(8,128)} copy(f32[16,147,768]{2,0,1:T(8,128)} %get-tuple-element.349) | data formatting | bytes 14450688 | tf_op jit(solution)/shard_map/add | solution.py:161
  262.5 26.4 %all_gather.23 = bf16[12,64]{0,1:T(8,128)(2,1)S(1)} all-gather(bf16[12,8]{0,1:T(8,128)(2,1)S(1)} %convert_element_type.232), channel_id=1, replica_groups=mesh['dp'=8,'mp'=4] {'dp'}, dimensions={1}, use_global_device_ids=true | all-gather | bytes 1728 | tf_op jit(solution)/shard_map/all_gather | solution.py:147
  345.1 20.1 %multiply_convert_fusion.2 = (bf16[2352,768]{1,0:T(8,128)(2,1)}, f32[2352,768]{1,0:T(8,128)S(1)}, f32[2352,768]{1,0:T(8,128)S(1)}) fusion(f32[768]{0:T(1024)} %reshape.311, bf16[2352,768]{1,0:T(8,128)(2,1)} %add_convert_fusion.1, bf16[768,768]{1,0:T(8,128)(2,1)} %all-gather.3.cloned.1.call-done), kind=kOutput, calls=%fused_computation.31 | convolution fusion | flops 2893750272 | bytes 22858752 | tf_op jit(solution)/shard_map/dot_general | solution.py:192
  365.2 8.8 %fusion.91 = (bf16[768]{0:T(1024)(128)(2,1)}, bf16[2352,768]{1,0:T(8,128)(2,1)S(1)}) fusion(f32[2352,768]{1,0:T(8,128)S(1)} %get-tuple-element.345, bf16[768,768]{0,1:T(8,128)(2,1)} %constant_dynamic-update-slice_fusion.6, f32[2352,768]{1,0:T(8,128)} %reshape.304, f32[2352]{0:T(1024)S(1)} %copy-done.26, f32[2352,768]{1,0:T(8,128)S(1)} %get-tuple-element.369, ...), kind=kOutput, calls=%fused_computation.199 | convolution fusion | flops 2807045376 | bytes 26482368 | tf_op jit(solution)/shard_map/dot_general | solution.py:95
  387.3 66.6 %all-reduce.7.cloned.1.call-done = bf16[2352,768]{1,0:T(8,128)(2,1)} async-done(((bf16[2352,768]{1,0:T(8,128)(2,1)}), bf16[2352,768]{1,0:T(8,128)(2,1)}) %all-reduce.7.cloned.1.call-update) | async-done | bytes 3612688 | tf_op jit(solution)/shard_map/psum | solution.py:217
  453.9 7.8 fusion.10
  461.7 7.6 fusion.82
  486.4 7.2 multiply_reduce_fusion
  522.6 7.4 convolution_convert_fusion.6
  536.1 8.6 %convolution_convert_fusion.5 = bf16[768,768]{0,1:T(8,128)(2,1)} fusion(bf16[2352,768]{1,0:T(8,128)(2,1)} %get-tuple-element.344, f32[2352,768]{1,0:T(8,128)} %reshape.304, f32[2352]{0:T(1024)S(1)} %copy-done.28), kind=kOutput, calls=%fused_computation.83 | convolution fusion | flops 2778734592 | bytes 12027072 | tf_op jit(solution)/shard_map/dot_general | solution.py:89
  544.7 19.5 %all-to-all-done.2 = bf16[8,96,768]{2,1,0:T(8,128)(2,1)S(1)} async-done(((bf16[8,96,768]{2,1,0:T(8,128)(2,1)}), bf16[8,96,768]{2,1,0:T(8,128)(2,1)S(1)}, u32[]{:S(2)}, u32[]{:S(2)}) %all-to-all-start.2) | async-done | bytes 1179680 | tf_op jit(solution)/shard_map/all_to_all | solution.py:44
  568.0 7.3 convolution_convert_fusion.1
  635.6 18.1 %all-to-all-done = bf16[8,96,3,192]{1,3,2,0:T(8,128)(2,1)} async-done(((bf16[8,96,3,192]{1,3,2,0:T(8,128)(2,1)}), bf16[8,96,3,192]{1,3,2,0:T(8,128)(2,1)}, u32[]{:S(2)}, u32[]{:S(2)}) %all-to-all-start) | async-done | bytes 884768 | tf_op jit(solution)/shard_map/all_to_all | solution.py:44
  661.3 54.7 %all-reduce.9.cloned.1.call-done = (bf16[2352,768]{1,0:T(8,128)(2,1)}, bf16[2352,768]{1,0:T(8,128)(2,1)}) async-done(((bf16[2352,768]{1,0:T(8,128)(2,1)}, bf16[2352,768]{1,0:T(8,128)(2,1)}), (bf16[2352,768]{1,0:T(8,128)(2,1)}, bf16[2352,768]{1,0:T(8,128)(2,1)})) %all-reduce.9.cloned.1.call-update) | async-done | bytes 7225360 | tf_op jit(solution)/shard_map/psum | solution.py:197
  718.7 7.2 fusion.15
  732.6 11.5 %fusion.13 = f32[2352,768]{1,0:T(8,128)} fusion(f32[2352,768]{1,0:T(8,128)} %copy-done.2, bf16[2352,768]{1,0:T(8,128)(2,1)} %get-tuple-element.309, f32[2352,768]{1,0:T(8,128)} %reshape.301, f32[2352]{0:T(1024)S(1)} %broadcast_multiply_fusion.1, f32[2352]{0:T(1024)S(1)} %div.112, f32[2352]{0:T(1024)S(1)} %broadcast_multiply_fusion.2, f32[768]{0:T(1024)S(1)} %copy-done.31, ...), kind=kLoop, calls=%fused_computation.22 | loop fusion | flops 16257024 | bytes 25329408 | tf_op jit(solution)/shard_map/add | solution.py:262
  760.8 8.5 %copy.396 = f32[16,147,768]{2,0,1:T(8,128)} copy(f32[16,147,768]{2,1,0:T(8,128)} %reshape.306) | data formatting | bytes 14450688
  (313 shorter events, 300.8 us)
Async XLA Ops:
  8.0 326.2 %all-reduce.5.cloned.1.call-start = ((), (), s32[]{:S(2)}) async-start(), calls=%async_computation.7 | async-start | bytes 7225344 | tf_op jit(solution)/shard_map/psum | solution.py:188
  37.5 85.5 %copy-start.30 = (f32[768]{0:T(1024)}, f32[768]{0:T(1024)S(1)}, u32[]{:S(2)}) copy-start(f32[768]{0:T(1024)S(1)} %get-tuple-element.307) | copy-start | bytes 9220
  138.3 33.1 %copy-start.17 = (f32[192,96]{1,0:T(8,128)S(1)}, f32[192,96]{1,0:T(8,128)}, u32[]{:S(2)}) copy-start(f32[192,96]{1,0:T(8,128)} %param.30) | copy-start | bytes 221188
  171.3 55.9 %copy-start.35 = (f32[1,3,64]{2,1,0:T(4,128)}, f32[1,3,64]{2,1,0:T(4,128)S(1)}, u32[]{:S(2)}) copy-start(f32[1,3,64]{2,1,0:T(4,128)S(1)} %copy.357) | copy-start | bytes 2308
  171.4 54.1 %copy-start.33 = (f32[1,3,64]{2,1,0:T(4,128)}, f32[1,3,64]{2,1,0:T(4,128)S(1)}, u32[]{:S(2)}) copy-start(f32[1,3,64]{2,1,0:T(4,128)S(1)} %copy.359) | copy-start | bytes 2308
  241.7 103.4 %all-gather.3.cloned.1.call-start = ((), (), s32[]{:S(2)}) async-start(), calls=%async_computation.8 | async-start | bytes 1327104 | tf_op jit(solution)/shard_map/all_gather | solution.py:144
  244.6 65.1 %collective-permute-start = (bf16[768,96]{0,1:T(8,128)(2,1)}, bf16[768,96]{0,1:T(8,128)(2,1)}, u32[]{:S(2)}, u32[]{:S(2)}) collective-permute-start(bf16[768,96]{0,1:T(8,128)(2,1)} %get-tuple-element.343), channel_id=1, source_target_pairs={{0,4},{4,8},{8,12},{12,16},{16,20},{20,24},{24,28},{28,0},{1,5},{5... | collective-permute-start | bytes 442376 | tf_op jit(solution)/shard_map/ppermute | solution.py:26
  245.2 64.4 %collective-permute-start.1 = (bf16[768,96]{0,1:T(8,128)(2,1)}, bf16[768,96]{0,1:T(8,128)(2,1)}, u32[]{:S(2)}, u32[]{:S(2)}) collective-permute-start(bf16[768,96]{0,1:T(8,128)(2,1)} %get-tuple-element.343), channel_id=1, source_target_pairs={{0,28},{4,0},{8,4},{12,8},{16,12},{20,16},{24,20},{28,24},{1,29},{... | collective-permute-start | bytes 442376 | tf_op jit(solution)/shard_map/ppermute | solution.py:29
  251.0 203.0 %all-reduce.7.cloned.1.call-start = ((), (), s32[]{:S(2)}) async-start(), calls=%async_computation.9 | async-start | bytes 7225344 | tf_op jit(solution)/shard_map/psum | solution.py:217
  309.7 8.1 %collective-permute-start.2 = (bf16[768,96]{0,1:T(8,128)(2,1)}, bf16[768,96]{0,1:T(8,128)(2,1)S(1)}, u32[]{:S(2)}, u32[]{:S(2)}) collective-permute-start(bf16[768,96]{0,1:T(8,128)(2,1)} %collective-permute-done), channel_id=1, source_target_pairs={{0,4},{4,8},{8,12},{12,16},{16,20},{20,24},{24,28},{28,0},{1,5},{5... | collective-permute-start | bytes 442376 | tf_op jit(solution)/shard_map/ppermute | solution.py:26
  309.7 8.0 %collective-permute-start.3 = (bf16[768,96]{0,1:T(8,128)(2,1)}, bf16[768,96]{0,1:T(8,128)(2,1)S(1)}, u32[]{:S(2)}, u32[]{:S(2)}) collective-permute-start(bf16[768,96]{0,1:T(8,128)(2,1)} %collective-permute-done.1), channel_id=1, source_target_pairs={{0,28},{4,0},{8,4},{12,8},{16,12},{20,16},{24,20},{28,24},{1,29},{... | collective-permute-start | bytes 442376 | tf_op jit(solution)/shard_map/ppermute | solution.py:29
  317.7 7.8 %collective-permute-start.4 = (bf16[768,96]{0,1:T(8,128)(2,1)S(1)}, bf16[768,96]{0,1:T(8,128)(2,1)S(1)}, u32[]{:S(2)}, u32[]{:S(2)}) collective-permute-start(bf16[768,96]{0,1:T(8,128)(2,1)S(1)} %collective-permute-done.2), channel_id=1, source_target_pairs={{0,4},{4,8},{8,12},{12,16},{16,20},{20,24},{24,28},{28,0},{1,5},{5... | collective-permute-start | bytes 442376 | tf_op jit(solution)/shard_map/ppermute | solution.py:26
  317.7 8.7 %collective-permute-start.5 = (bf16[768,96]{0,1:T(8,128)(2,1)S(1)}, bf16[768,96]{0,1:T(8,128)(2,1)S(1)}, u32[]{:S(2)}, u32[]{:S(2)}) collective-permute-start(bf16[768,96]{0,1:T(8,128)(2,1)S(1)} %collective-permute-done.3), channel_id=1, source_target_pairs={{0,28},{4,0},{8,4},{12,8},{16,12},{20,16},{24,20},{28,24},{1,29},{... | collective-permute-start | bytes 442376 | tf_op jit(solution)/shard_map/ppermute | solution.py:29
  325.6 8.0 %collective-permute-start.6 = (bf16[768,96]{0,1:T(8,128)(2,1)S(1)}, bf16[768,96]{0,1:T(8,128)(2,1)S(1)}, u32[]{:S(2)}, u32[]{:S(2)}) collective-permute-start(bf16[768,96]{0,1:T(8,128)(2,1)S(1)} %collective-permute-done.4), channel_id=1, source_target_pairs={{0,4},{4,8},{8,12},{12,16},{16,20},{20,24},{24,28},{28,0},{1,5},{5... | collective-permute-start | bytes 442376 | tf_op jit(solution)/shard_map/ppermute | solution.py:26
  383.2 133.7 %all-to-all-start.5 = ((bf16[8,12,8]{1,2,0:T(8,128)(2,1)}), bf16[8,12,8]{1,2,0:T(8,128)(2,1)}, u32[]{:S(2)}, u32[]{:S(2)}) async-start(bf16[8,12,8]{1,2,0:T(8,128)(2,1)} %copy.382), calls=%async_computation.5 | async-start | bytes 32768 | tf_op jit(solution)/shard_map/all_to_all | solution.py:44
  516.9 13.2 %all-to-all-start.4 = ((bf16[8,2,3,8]{3,1,2,0:T(2,128)(2,1)}), bf16[8,2,3,8]{3,1,2,0:T(2,128)(2,1)S(1)}, u32[]{:S(2)}, u32[]{:S(2)}) async-start(bf16[8,2,3,8]{3,1,2,0:T(2,128)(2,1)} %copy.379), calls=%async_computation.4 | async-start | bytes 24576 | tf_op jit(solution)/shard_map/all_to_all | solution.py:44
  530.0 34.1 %all-to-all-start.2 = ((bf16[8,96,768]{2,1,0:T(8,128)(2,1)}), bf16[8,96,768]{2,1,0:T(8,128)(2,1)S(1)}, u32[]{:S(2)}, u32[]{:S(2)}) async-start(bf16[8,96,768]{2,1,0:T(8,128)(2,1)} %bitcast.18), calls=%async_computation.2 | async-start | bytes 2359296 | tf_op jit(solution)/shard_map/all_to_all | solution.py:44
  564.1 37.6 %all-to-all-start.3 = ((bf16[8,768,96]{1,2,0:T(8,128)(2,1)}), bf16[8,768,96]{1,2,0:T(8,128)(2,1)S(1)}, u32[]{:S(2)}, u32[]{:S(2)}) async-start(bf16[8,768,96]{1,2,0:T(8,128)(2,1)} %bitcast.97), calls=%async_computation.3 | async-start | bytes 2359296 | tf_op jit(solution)/shard_map/all_to_all | solution.py:44
  567.7 148.3 %all-reduce.9.cloned.1.call-start = ((), (), s32[]{:S(2)}) async-start(), calls=%async_computation.10 | async-start | bytes 14450688 | tf_op jit(solution)/shard_map/psum | solution.py:197
  601.7 18.3 %all-to-all-start.1 = ((bf16[8,192,96]{2,1,0:T(8,128)(2,1)}), bf16[8,192,96]{2,1,0:T(8,128)(2,1)S(1)}, u32[]{:S(2)}, u32[]{:S(2)}) async-start(bf16[8,192,96]{2,1,0:T(8,128)(2,1)} %bitcast.91), calls=%async_computation.1 | async-start | bytes 786432 | tf_op jit(solution)/shard_map/all_to_all | solution.py:44
  620.0 33.8 %all-to-all-start = ((bf16[8,96,3,192]{1,3,2,0:T(8,128)(2,1)}), bf16[8,96,3,192]{1,3,2,0:T(8,128)(2,1)}, u32[]{:S(2)}, u32[]{:S(2)}) async-start(bf16[8,96,3,192]{1,3,2,0:T(8,128)(2,1)} %copy.376), calls=%async_computation | async-start | bytes 2359296 | tf_op jit(solution)/shard_map/all_to_all | solution.py:44
  631.6 87.1 %copy-start.31 = (f32[768]{0:T(1024)S(1)}, f32[768]{0:T(1024)}, u32[]{:S(2)}) copy-start(f32[768]{0:T(1024)} %copy-done.30) | copy-start | bytes 9220
  633.9 92.0 %copy-start.19 = (f32[192,96]{1,0:T(8,128)}, f32[192,96]{1,0:T(8,128)S(1)}, u32[]{:S(2)}) copy-start(f32[192,96]{1,0:T(8,128)S(1)} %convert_reduce_fusion.3) | copy-start | bytes 221188
  726.7 42.6 %all-to-all-start.6 = ((bf16[8,6,96]{2,1,0:T(8,128)(2,1)}), bf16[8,6,96]{2,1,0:T(8,128)(2,1)S(1)}, u32[]{:S(2)}, u32[]{:S(2)}) async-start(bf16[8,6,96]{2,1,0:T(8,128)(2,1)} %copy.384), calls=%async_computation.6 | async-start | bytes 32768 | tf_op jit(solution)/shard_map/all_to_all | solution.py:44
  (59 other events, 579.6 us)
Sparse Core Ops, SparseCore 0:
  241.8 76.3 all-reduce.4
  380.5 73.4 all-reduce.6
  580.5 135.4 all-reduce.8
Sparse Core Ops, SparseCore 1:
  251.0 38.5 all-gather.2
